TPU v7x, 32 devices: a whole 2x2x4 slice. The times are simulated.
32 devices in a mesh: az: 4 (over x, core), rad: 8 (over z, y).
Axes of the slice: x: 2, y: 2, z: 4, core: 2. Of those that a mesh axis runs over, the one named last changes fastest.
Arguments:
- fields: float32 [4, 16, 64, 512], P(None, None, 'rad', 'az'), may hold values from -6 to 6, as said below
- shifts: int32 [16, 64], P(None, 'rad'), may hold values from 0 to 511, as said below
- courant: float32 [16, 64], P(None, 'rad'), may hold values from -0.45 to 0.45
Outputs:
- advanced: float32 [4, 16, 64, 512], P(None, None, 'rad', 'az')
Inputs may be any that keep to these rules, and one draw needn't show every extreme that they name: fields 0 and 1 (velocities) lie in the range; fields 2 and 3 (energy, density) lie between 0.5 and 2. `shifts`: any whole shift of a cycle in cells.
All inputs are finite; a program needn't handle non-finite values.
Results may differ from a plain program's by a relative error of at most 0.0003.
Values sent between devices are 32-bit elements; how exact they have to be, the bound alone decides.
A program may use at most 64 MiB of HBM per device.

v0:
```python
import functools
import math

import jax
import jax.numpy as jnp
from jax import lax
from jax.experimental import pallas as pl
from jax.experimental.pallas import tpu as pltpu
from jax.sharding import PartitionSpec as P

inner_radius = 0.4
adiabatic = 1.4
MESH = pl.DeviceIdType.MESH
OFFSETS = (-2, -1, 0, 1)
CHUNKS = 4


def remote(src, dst, send, recv, az, rad):
    return pltpu.make_async_remote_copy(
        src_ref=src,
        dst_ref=dst,
        send_sem=send,
        recv_sem=recv,
        device_id={"az": az, "rad": rad},
        device_id_type=MESH,
    )


def minmod(a, b):
    return jnp.maximum(jnp.minimum(a, b), 0.0) + jnp.minimum(jnp.maximum(a, b), 0.0)


def kernel(n, rn, fields, shifts_in, courant_in, out, G, H, SEG, LANE, CA, shifts, courant,
           local_sem, small_sem, xs, xr, hs, hr, cs, cr, fs, fr):
    _, T, R, L = fields.shape
    X = n // 2
    K = xs.shape[0]
    tc = T // K
    az = lax.axis_index("az")
    rad = lax.axis_index("rad")
    x, c = az // 2, az % 2
    mate = x * 2 + (1 - c)

    def column(k):
        return lax.rem(x + k, X) * 2 + c

    def source(k, core):
        return lax.rem(x + X - k, X) * 2 + core

    has_low, has_high = rad > 0, rad < rn - 1
    sends = (has_high, has_low)
    receives = (has_low, has_high)
    toward = (rad + 1, rad - 1)

    local = pltpu.make_async_copy(fields, G.at[az], local_sem)
    local.start()
    small = (
        pltpu.make_async_copy(shifts_in, shifts, small_sem.at[0]),
        pltpu.make_async_copy(courant_in, courant, small_sem.at[1]),
    )
    for copy in small:
        copy.start()

    barrier = pltpu.get_barrier_semaphore()

    def greet(a, r):
        pl.semaphore_signal(barrier, inc=1, device_id={"az": a, "rad": r}, device_id_type=MESH)

    greet(mate, rad)
    for k in range(1, X):
        greet(column(k), rad)
    for way in range(2):
        @pl.when(sends[way])
        def _():
            for k in range(X):
                greet(column(k), toward[way])
    neighbours = has_low.astype(jnp.int32) + has_high.astype(jnp.int32)


    pl.semaphore_wait(barrier, X + X * neighbours)

    def block(ref, seg, j):
        return ref.at[seg, :, pl.ds(j * tc, tc)]

    def field_copy(j, k):
        return remote(fields.at[:, pl.ds(j * tc, tc)], block(G, az, j), xs.at[j, k - 1], xr.at[j, k - 1], column(k), rad)

    def field_arrival(j, k):
        seg = source(k, c)
        return remote(block(G, seg, j), block(G, seg, j), xs.at[j, k - 1], xr.at[j, k - 1], column(k), rad)

    def edge_copy(way, k):
        return remote(fields.at[0:3, :, (R - 1) * (1 - way), :], H.at[way, az], hs.at[way, k], hr.at[way, k], column(k), toward[way])

    def edge_arrival(way, k):
        return remote(H.at[way, az], H.at[way, source(k, c)], hs.at[way, k], hr.at[way, k], column(k), rad)

    def mate_copy(j, k):
        seg = source(k, c)
        sent = block(G, seg, j) if k else fields.at[:, pl.ds(j * tc, tc)]
        return remote(sent, block(G, seg, j), cs.at[j, k], cr.at[j, k], mate, rad)

    def mate_arrival(j, k):
        seg = source(k, 1 - c)
        return remote(block(G, seg, j), block(G, seg, j), cs.at[j, k], cr.at[j, k], mate, rad)

    def mate_edge(way, k):
        seg = source(k, c)
        return remote(H.at[way, seg], H.at[way, seg], fs.at[way, k], fr.at[way, k], mate, rad)

    def mate_edge_arrival(way, k):
        seg = source(k, 1 - c)
        return remote(H.at[way, seg], H.at[way, seg], fs.at[way, k], fr.at[way, k], mate, rad)

    for way in range(2):
        @pl.when(sends[way])
        def _():
            for k in range(X - 1, -1, -1):
                edge_copy(way, k).start()
    for j in range(K):
        for k in range(1, X):
            field_copy(j, k).start()
    for j in range(K):
        mate_copy(j, 0).start()

    for way in range(2):
        @pl.when(jnp.logical_not(receives[way]))
        def _():
            H[way] = jnp.zeros(H.shape[1:], jnp.float32)

    phi_count, rad_count = n * L, rn * R
    phi_step = 2.0 * math.pi / phi_count
    rad_step = 1.0 / rad_count
    spacing = min(rad_step, inner_radius * phi_step)
    dt = 0.2 * spacing
    viscosity = 0.05 * spacing * spacing / dt
    row = lax.broadcasted_iota(jnp.int32, (R, L), 0)
    lane = lax.broadcasted_iota(jnp.int32, (R, L), 1)
    radius = inner_radius + ((rad * R + row).astype(jnp.float32) + 0.5) * (1.0 / rad_count)
    width = radius * phi_step
    inv_r = 1.0 / radius
    inv_w = 1.0 / width
    spread_az = (dt * viscosity) * inv_w * inv_w
    spread_rad = dt * viscosity / (rad_step * rad_step)
    press_rad = dt * (adiabatic - 1.0) * 0.5 / rad_step
    press_az = (dt * (adiabatic - 1.0) * 0.5) * inv_w
    turn = dt * inv_r
    pull = dt * inv_r * inv_r
    heat = dt * (adiabatic - 1.0)
    heat_rad = heat * 0.5 / rad_step
    heat_az = (heat * 0.5) * inv_w
    heat_r = heat * inv_r
    bits = L.bit_length() - 1

    local.wait()
    for copy in small:
        copy.wait()
    for t in range(T):
        moves = jnp.broadcast_to(shifts[:, t : t + 1], (R, L))
        cour = jnp.broadcast_to(courant[:, t : t + 1], (R, L))
        CA[t] = jnp.abs(cour)
        sign = jnp.where(cour >= 0.0, 1, -1)
        for o, offset in enumerate(OFFSETS):
            s = moves - sign * offset
            s = jnp.where(s < 0, s + phi_count, s)
            s = jnp.where(s >= phi_count, s - phi_count, s)
            q = s >> bits
            rest = s & (L - 1)
            seg = az - q - jnp.where(lane + rest >= L, 1, 0)
            SEG[t, o] = jnp.where(seg < 0, seg + n, seg)
            LANE[t, o] = (lane - rest) & (L - 1)

    first_lane, last_lane = lane == 0, lane == L - 1
    low_own = (row == 0) & jnp.logical_not(has_low)
    high_own = (row == R - 1) & jnp.logical_not(has_high)
    low_halo = (row == 0) & has_low
    high_halo = (row == R - 1) & has_high

    def step(t, carry):
        raw = [[G[s, f, t] for f in range(4)] for s in range(n)]
        moved = []
        for s in range(n):
            before, here, after = raw[s - 1], raw[s], raw[(s + 1) % n]
            vr, vp, en, den = here

            def around(f):
                q = here[f]
                left = pltpu.roll(jnp.where(last_lane, before[f], q), 1, 1)
                right = pltpu.roll(jnp.where(first_lane, after[f], q), L - 1, 1)
                low = jnp.where(low_own, q, pltpu.roll(q, 1, 0))
                low = jnp.where(low_halo, H[0, s, f, pl.ds(t, 1), :], low)
                high = jnp.where(high_own, q, pltpu.roll(q, R - 1, 0))
                high = jnp.where(high_halo, H[1, s, f, pl.ds(t, 1), :], high)
                return left, right, low, high

            vl, vh, vd, vu = around(0)
            pl_, ph, pd, pu = around(1)
            el, eh, ed, eu = around(2)
            inv_den = 1.0 / den
            new_r = vr + (
                spread_az * (vh + vl - 2.0 * vr)
                + spread_rad * (vu + vd - 2.0 * vr)
                + (vp * vp * turn - pull)
                - press_rad * (eu - ed) * inv_den
            )
            new_p = vp + (
                spread_az * (ph + pl_ - 2.0 * vp)
                + spread_rad * (pu + pd - 2.0 * vp)
                - vr * vp * turn
                - press_az * (eh - el) * inv_den
            )
            new_e = en - en * (heat_rad * (vu - vd) + heat_az * (ph - pl_) + heat_r * vr)
            moved.append((new_r, new_p, new_e, den))
        amount = CA[t]
        half = 0.5 * (1.0 - amount)
        taken = [[] for _ in range(4)]
        for o in range(len(OFFSETS)):
            seg, at = SEG[t, o], LANE[t, o]
            chosen = [seg == s for s in range(n - 1)]
            for f in range(4):
                value = moved[n - 1][f]
                for s in range(n - 1):
                    value = jnp.where(chosen[s], moved[s][f], value)
                taken[f].append(jnp.take_along_axis(value, at, axis=1, mode="promise_in_bounds"))
        for f in range(4):
            q0, q1, q2, q3 = taken[f]
            d0, d1, d2 = q1 - q0, q2 - q1, q3 - q2
            enters = q1 + half * minmod(d0, d1)
            leaves = q2 + half * minmod(d1, d2)
            out[f, t] = q2 - amount * (leaves - enters)
        return carry

    def finish(j):
        for k in range(X):
            mate_arrival(j, k).wait_recv()
        def group(i, carry):
            for u in range(2):
                carry = step(2 * i + u, carry)
            return carry

        lax.fori_loop(j * (tc // 2), (j + 1) * (tc // 2), group, 0)

    for way in range(2):
        @pl.when(receives[way])
        def _():
            for k in range(X):
                edge_arrival(way, k).wait_recv()
                mate_edge(way, k).start()

    def turn_over(j, carry):
        @pl.when(j < K)
        def _():
            for k in range(1, X):
                field_arrival(j, k).wait_recv()
                mate_copy(j, k).start()

        for way in range(2):
            @pl.when((j == 1) & receives[way])
            def _():
                for k in range(X):
                    mate_edge_arrival(way, k).wait_recv()

        @pl.when(j > 0)
        def _():
            finish(j - 1)

        return carry

    lax.fori_loop(0, K + 1, turn_over, 0)

    for way in range(2):
        @pl.when(sends[way])
        def _():
            for k in range(X):
                edge_copy(way, k).wait_send()

        @pl.when(receives[way])
        def _():
            for k in range(X):
                mate_edge(way, k).wait_send()
    for j in range(K):
        for k in range(1, X):
            field_copy(j, k).wait_send()
        for k in range(X):
            mate_copy(j, k).wait_send()


def shards(fields, shifts, courant):
    n, rn = lax.axis_size("az"), lax.axis_size("rad")
    F, T, R, L = fields.shape
    X = n // 2
    K = math.gcd(T, CHUNKS)
    held = (n + 2) * F * T * R * L + 2 * n * 3 * T * L + 9 * T * R * L
    grant = 4 * held + (2 << 20)
    dma = pltpu.SemaphoreType.DMA
    vmem = pl.BlockSpec(memory_space=pltpu.VMEM)
    return pl.pallas_call(
        functools.partial(kernel, n, rn),
        out_shape=jax.ShapeDtypeStruct(fields.shape, jnp.float32),
        in_specs=[pl.BlockSpec(memory_space=pltpu.HBM)] * 3,
        out_specs=vmem,
        scratch_shapes=[
            pltpu.VMEM((n, F, T, R, L), jnp.float32),
            pltpu.VMEM((2, n, 3, T, L), jnp.float32),
            pltpu.VMEM((T, 4, R, L), jnp.int32),
            pltpu.VMEM((T, 4, R, L), jnp.int32),
            pltpu.VMEM((T, R, L), jnp.float32),
            pltpu.VMEM((R, T), jnp.int32),
            pltpu.VMEM((R, T), jnp.float32),
            dma(()), dma((2,)),
            dma((K, X - 1)), dma((K, X - 1)),
            dma((2, X)), dma((2, X)),
            dma((K, X)), dma((K, X)),
            dma((2, X)), dma((2, X)),
        ],
        compiler_params=pltpu.CompilerParams(collective_id=0, has_side_effects=True, vmem_limit_bytes=grant),
    )(*(pltpu.with_memory_space_constraint(v, pltpu.HBM) for v in (fields, shifts.T, courant.T)))


def solution(mesh):
    return jax.shard_map(
        shards,
        mesh=mesh,
        in_specs=(P(None, None, "rad", "az"), P(None, "rad"), P(None, "rad")),
        out_specs=P(None, None, "rad", "az"),
        check_vma=False,
    )
```

profile of v0, /device:TPU:1, one launch (start us, length us, event | category | flops | bytes accessed | tf_op | source)
XLA Modules:
  0.0 14.2 jit_solution(3156237168431457172)
XLA Ops:
  0.0 13.5 %shard_map.37 = f32[4,16,8,128]{3,2,1,0:T(8,128)S(1)} custom-call(f32[4,16,8,128]{3,2,1,0:T(8,128)} %fields.1, s32[8,16]{1,0:T(8,128)} %bitcast.2, f32[8,16]{1,0:T(8,128)} %bitcast.3), custom_call_target="tpu_custom_call" | custom-call | tf_op jit(solution)/shard_map/pallas_call | solution.py:297
  13.5 0.7 %copy.5 = f32[4,16,8,128]{3,2,1,0:T(8,128)} copy(f32[4,16,8,128]{3,2,1,0:T(8,128)S(1)} %shard_map.37) | data formatting | bytes 524288
where the time goes:
time: 14.3 us; the launch traced here: 14.2 us
  Pallas kernels  13.5 us (94%)
  local copies, waits for them, and re-layouts  0.71 us (5%)
    pallas_call x1, Pallas kernels, shards(): pl.pallas_call(functools.partial(kernel, n, rn), out_shape=jax.ShapeDtype...  13.5 us
    unnamed x1, local copies, waits for them, and re-layouts  0.71 us

commit v1 on v0

v1 whole, which is shorter than its diff:
```python
import functools
import math

import jax
import jax.numpy as jnp
from jax import lax
from jax.experimental import pallas as pl
from jax.experimental.pallas import tpu as pltpu
from jax.sharding import PartitionSpec as P

inner_radius = 0.4
adiabatic = 1.4
MESH = pl.DeviceIdType.MESH
OFFSETS = (-2, -1, 0, 1)
BOUNDS = (0, 4, 9, 13, 15, 16)


def remote(src, dst, send, recv, az, rad):
    return pltpu.make_async_remote_copy(
        src_ref=src,
        dst_ref=dst,
        send_sem=send,
        recv_sem=recv,
        device_id={"az": az, "rad": rad},
        device_id_type=MESH,
    )


def minmod(a, b):
    return jnp.maximum(jnp.minimum(a, b), 0.0) + jnp.minimum(jnp.maximum(a, b), 0.0)


def kernel(n, rn, bounds, fields, shifts_in, courant_in, out, raw, early, G, H, ZS, ZR, FX, SEG, LANE, CA, shifts, courant,
           local_sem, small_sem, sent, edge_sent, edge_got, side_sent, side_got, fix_sent, fix_got, dens_got, dens_mate, got, mate_got):
    _, T, R, L = fields.shape
    X = n // 2
    K = len(bounds) - 1
    fill = bounds[1]
    az = lax.axis_index("az")
    rad = lax.axis_index("rad")
    x, c = az // 2, az % 2
    mate = x * 2 + (1 - c)
    before, after = lax.rem(az + n - 1, n), lax.rem(az + 1, n)

    def column(k, core=None):
        return lax.rem(x + k, X) * 2 + (c if core is None else core)

    def source(k, core):
        return lax.rem(x + X - k, X) * 2 + core

    has_low, has_high = rad > 0, rad < rn - 1
    sends = (has_high, has_low)
    receives = (has_low, has_high)
    toward = (rad + 1, rad - 1)

    barrier = pltpu.get_barrier_semaphore()

    def greet(a, r):
        pl.semaphore_signal(barrier, inc=1, device_id={"az": a, "rad": r}, device_id_type=MESH)

    greet(mate, rad)
    for k in range(1, X):
        greet(column(k), rad)
        greet(column(k, 1 - c), rad)
    for way in range(2):
        @pl.when(sends[way])
        def _():
            greet(az, toward[way])

    small = (
        pltpu.make_async_copy(shifts_in, shifts, small_sem.at[0]),
        pltpu.make_async_copy(courant_in, courant, small_sem.at[1]),
    )
    local = (
        pltpu.make_async_copy(fields.at[0:3], raw, local_sem.at[0]),
        pltpu.make_async_copy(fields.at[3], G.at[az, 3], local_sem.at[1]),
    )
    for copy in small + local:
        copy.start()

    phi_count, rad_count = n * L, rn * R
    phi_step = 2.0 * math.pi / phi_count
    rad_step = 1.0 / rad_count
    spacing = min(rad_step, inner_radius * phi_step)
    dt = 0.2 * spacing
    viscosity = 0.05 * spacing * spacing / dt
    row = lax.broadcasted_iota(jnp.int32, (R, L), 0)
    lane = lax.broadcasted_iota(jnp.int32, (R, L), 1)
    radius = inner_radius + ((rad * R + row).astype(jnp.float32) + 0.5) * (1.0 / rad_count)
    width = radius * phi_step
    inv_r = 1.0 / radius
    inv_w = 1.0 / width
    spread_az = (dt * viscosity) * inv_w * inv_w
    spread_rad = dt * viscosity / (rad_step * rad_step)
    press_rad = dt * (adiabatic - 1.0) * 0.5 / rad_step
    press_az = (dt * (adiabatic - 1.0) * 0.5) * inv_w
    turn = dt * inv_r
    pull = dt * inv_r * inv_r
    heat = dt * (adiabatic - 1.0)
    heat_rad = heat * 0.5 / rad_step
    heat_az = (heat * 0.5) * inv_w
    heat_r = heat * inv_r
    bits = L.bit_length() - 1
    first_lane, last_lane = lane == 0, lane == L - 1
    first_row, last_row = row == 0, row == R - 1

    def turned(value, amount):
        return pltpu.roll(value, amount % L, 1) if amount % L else value

    for copy in small:
        copy.wait()
    for t in range(T):
        moves = jnp.broadcast_to(shifts[:, t : t + 1], (R, L))
        cour = jnp.broadcast_to(courant[:, t : t + 1], (R, L))
        CA[t] = jnp.abs(cour)
        sign = jnp.where(cour >= 0.0, 1, -1)
        for o, offset in enumerate(OFFSETS):
            s = moves - sign * offset
            s = jnp.where(s < 0, s + phi_count, s)
            s = jnp.where(s >= phi_count, s - phi_count, s)
            q = s >> bits
            rest = s & (L - 1)
            seg = az - q - jnp.where(lane + rest >= L, 1, 0)
            SEG[t, o] = jnp.where(seg < 0, seg + n, seg)
            LANE[t, o] = (lane - rest) & (L - 1)

    for copy in local:
        copy.wait()

    for side in range(2):
        for p in range(ZS.shape[1]):
            packed = jnp.zeros((R, L), jnp.float32)
            for i in range(p * L, min(3 * T, (p + 1) * L)):
                packed = jnp.where(lane == i - p * L, turned(raw[i // T, i % T], i - p * L + side), packed)
            ZS[side, p] = packed

    for way in range(2):
        @pl.when(jnp.logical_not(receives[way]))
        def _():
            H[way] = raw[:, :, (R - 1) * way, :]

    def stencil(t, dst, inner):
        vr, vp, en, den = raw[0, t], raw[1, t], raw[2, t], G[az, 3, t]

        def around(f, q):
            i = f * T + t
            left, right = turned(q, 1), turned(q, L - 1)
            low, high = pltpu.roll(q, 1, 0), pltpu.roll(q, R - 1, 0)
            if not inner:
                left = jnp.where(first_lane, turned(ZR[0, i // L], -i), left)
                right = jnp.where(last_lane, turned(ZR[1, i // L], L - 1 - i), right)
                low = jnp.where(first_row, H[0, f, pl.ds(t, 1), :], low)
                high = jnp.where(last_row, H[1, f, pl.ds(t, 1), :], high)
            return left, right, low, high

        vl, vh, vd, vu = around(0, vr)
        pl_, ph, pd, pu = around(1, vp)
        el, eh, ed, eu = around(2, en)
        inv_den = 1.0 / den
        dst[0, t] = vr + (
            spread_az * (vh + vl - 2.0 * vr)
            + spread_rad * (vu + vd - 2.0 * vr)
            + (vp * vp * turn - pull)
            - press_rad * (eu - ed) * inv_den
        )
        dst[1, t] = vp + (
            spread_az * (ph + pl_ - 2.0 * vp)
            + spread_rad * (pu + pd - 2.0 * vp)
            - vr * vp * turn
            - press_az * (eh - el) * inv_den
        )
        dst[2, t] = en - en * (heat_rad * (vu - vd) + heat_az * (ph - pl_) + heat_r * vr)

    for t in range(fill):
        stencil(t, early, True)

    neighbours = has_low.astype(jnp.int32) + has_high.astype(jnp.int32)
    pl.semaphore_wait(barrier, 2 * X - 1 + neighbours)

    def side_copy(side):
        return remote(ZS.at[side], ZR.at[1 - side], side_sent, side_got, after if side else before, rad)

    def edge_copy(way):
        return remote(raw.at[:, :, (R - 1) * (1 - way), :], H.at[way], edge_sent.at[way], edge_got.at[way], az, toward[way])

    def block(seg, j):
        return G.at[seg, 0:3, pl.ds(bounds[j], bounds[j + 1] - bounds[j])]

    for side in range(2):
        side_copy(side).start()
    for way in range(2):
        @pl.when(sends[way])
        def _():
            edge_copy(way).start()
    for k in range(1, X):
        remote(G.at[az, 3], G.at[az, 3], sent, dens_got.at[k - 1], column(k), rad).start()
    for k in range(1, X):
        inside = pl.ds(1, R - 2)
        remote(early.at[:, :, inside], G.at[az, 0:3, pl.ds(0, fill), inside], sent, got.at[0, k - 1], column(k), rad).start()
    remote(G.at[az, 3], G.at[az, 3], sent, dens_mate, mate, rad).start()

    remote(ZR, ZR, side_sent, side_got, mate, rad).wait_recv()
    for way in range(2):
        @pl.when(receives[way])
        def _():
            remote(H.at[way], H.at[way], edge_sent.at[way], edge_got.at[way], az, rad).wait_recv()

    for j in [1, 0] + list(range(2, K)):
        for t in range(bounds[j], bounds[j + 1]):
            stencil(t, G.at[az], False)
        if j == 0:
            for p in range(FX.shape[1]):
                packed = jnp.zeros((R, L), jnp.float32)
                for i in range(p * L, min(6 * fill, (p + 1) * L)):
                    f, t, side = i // (2 * fill), i // 2 % fill, i % 2
                    packed = jnp.where(lane == i - p * L, turned(G[az, f, t], i - p * L + side), packed)
                FX[az, p] = packed
            for k in range(1, X):
                for r in (0, R - 1):
                    line = G.at[az, 0:3, pl.ds(0, fill), r]
                    remote(line, line, sent, got.at[0, k - 1], column(k), rad).start()
                remote(FX.at[az], FX.at[az], fix_sent, fix_got.at[k - 1], column(k), rad).start()
        else:
            for k in range(1, X):
                remote(block(az, j), block(az, j), sent, got.at[j, k - 1], column(k), rad).start()
                if j == K - 1:
                    remote(block(az, j), block(az, j), sent, mate_got.at[j], column(k, 1 - c), rad).start()
        remote(block(az, j), block(az, j), sent, mate_got.at[j], mate, rad).start()

    def step(t):
        amount = CA[t]
        half = 0.5 * (1.0 - amount)
        taken = [[] for _ in range(4)]
        moved = [[G[s, f, t] for f in range(4)] for s in range(n)]
        for o in range(len(OFFSETS)):
            seg, at = SEG[t, o], LANE[t, o]
            chosen = [seg == s for s in range(n - 1)]
            for f in range(4):
                value = moved[n - 1][f]
                for s in range(n - 1):
                    value = jnp.where(chosen[s], moved[s][f], value)
                taken[f].append(jnp.take_along_axis(value, at, axis=1, mode="promise_in_bounds"))
        for f in range(4):
            q0, q1, q2, q3 = taken[f]
            d0, d1, d2 = q1 - q0, q2 - q1, q3 - q2
            enters = q1 + half * minmod(d0, d1)
            leaves = q2 + half * minmod(d1, d2)
            out[f, t] = q2 - amount * (leaves - enters)

    def take(j):
        for k in range(1, X):
            seg = source(k, c)
            copy = remote(block(seg, j), block(seg, j), sent, got.at[j, k - 1], mate, rad)
            copy.wait_recv()
            if j == 0:
                remote(FX.at[seg], FX.at[seg], fix_sent, fix_got.at[k - 1], mate, rad).wait_recv()
                for i in range(3 * fill):
                    f, t = i // fill, i % fill
                    p, at = 2 * i // L, 2 * i % L
                    value = jnp.where(first_lane, turned(FX[seg, p], -at), G[seg, f, t])
                    G[seg, f, t] = jnp.where(last_lane, turned(FX[seg, p], L - 2 - at), value)
            if j < K - 1:
                remote(block(seg, j), block(seg, j), sent, mate_got.at[j], mate, rad).start()

    def finish(j):
        every = G.at[pl.ds(0, X), 0:3, pl.ds(0, bounds[j + 1] - bounds[j])]
        remote(every, every, sent, mate_got.at[j], mate, rad).wait_recv()

        for t in range(bounds[j], bounds[j + 1]):
            step(t)

    for k in range(1, X):
        seg = source(k, c)
        copy = remote(G.at[seg, 3], G.at[seg, 3], sent, dens_got.at[k - 1], mate, rad)
        copy.wait_recv()
        remote(G.at[seg, 3], G.at[seg, 3], sent, dens_mate, mate, rad).start()
    take(1)
    take(0)
    dens = G.at[pl.ds(0, X), 3]
    remote(dens, dens, sent, dens_mate, mate, rad).wait_recv()
    order = [1, 0] + list(range(2, K))
    for i, j in enumerate(order):
        if i > 0 and i + 1 < K:
            take(order[i + 1])
        finish(j)

    for way in range(2):
        @pl.when(sends[way])
        def _():
            edge_copy(way).wait_send()
    remote(ZS, ZS, side_sent, side_got, mate, rad).wait_send()
    fixes = FX.at[pl.ds(0, X - 1)]
    remote(fixes, fixes, fix_sent, side_got, mate, rad).wait_send()
    every = G.at[pl.ds(0, 2 * X - 1)]
    remote(every, every, sent, side_got, mate, rad).wait_send()


def shards(fields, shifts, courant):
    n, rn = lax.axis_size("az"), lax.axis_size("rad")
    F, T, R, L = fields.shape
    X = n // 2
    bounds = sorted({T * b // BOUNDS[-1] for b in BOUNDS})
    K, fill = len(bounds) - 1, bounds[1]
    packs, fixes = -(-3 * T // L), -(-6 * fill // L)
    tile = R * L
    held = (n + 2) * F * T * tile + 3 * fill * tile + 2 * 3 * T * L + (4 * packs + n * fixes) * tile + 9 * T * tile
    grant = 4 * held + (2 << 20)
    dma = pltpu.SemaphoreType.DMA
    vmem = pl.BlockSpec(memory_space=pltpu.VMEM)
    return pl.pallas_call(
        functools.partial(kernel, n, rn, bounds),
        out_shape=jax.ShapeDtypeStruct(fields.shape, jnp.float32),
        in_specs=[pl.BlockSpec(memory_space=pltpu.HBM)] * 3,
        out_specs=vmem,
        scratch_shapes=[
            pltpu.VMEM((3, T, R, L), jnp.float32),
            pltpu.VMEM((3, fill, R, L), jnp.float32),
            pltpu.VMEM((n, F, T, R, L), jnp.float32),
            pltpu.VMEM((2, 3, T, L), jnp.float32),
            pltpu.VMEM((2, packs, R, L), jnp.float32),
            pltpu.VMEM((2, packs, R, L), jnp.float32),
            pltpu.VMEM((n, fixes, R, L), jnp.float32),
            pltpu.VMEM((T, 4, R, L), jnp.int32),
            pltpu.VMEM((T, 4, R, L), jnp.int32),
            pltpu.VMEM((T, R, L), jnp.float32),
            pltpu.VMEM((R, T), jnp.int32),
            pltpu.VMEM((R, T), jnp.float32),
            dma((2,)), dma((2,)),
            dma(()), dma((2,)), dma((2,)), dma(()), dma(()), dma(()), dma((X - 1,)),
            dma((X - 1,)), dma(()), dma((K, X - 1)), dma((K,)),
        ],
        compiler_params=pltpu.CompilerParams(collective_id=0, has_side_effects=True, vmem_limit_bytes=grant),
    )(*(pltpu.with_memory_space_constraint(v, pltpu.HBM) for v in (fields, shifts.T, courant.T)))


def solution(mesh):
    return jax.shard_map(
        shards,
        mesh=mesh,
        in_specs=(P(None, None, "rad", "az"), P(None, "rad"), P(None, "rad")),
        out_specs=P(None, None, "rad", "az"),
        check_vma=False,
    )
```

time: 14.3 us -> 14.1 us (0.986)
  the two profiles are of different devices: /device:TPU:1 before, /device:TPU:0 now
where the time goes in v1:
time: 14.1 us; the launch traced here: 14 us
  Pallas kernels  13.2 us (94%)
  local copies, waits for them, and re-layouts  0.71 us (5%)
    pallas_call x1, Pallas kernels, shards(): pl.pallas_call(functools.partial(kernel, n, rn, bounds), out_shape=jax.Sh...  13.2 us
    unnamed x1, local copies, waits for them, and re-layouts  0.71 us

profile of v1, /device:TPU:0, one launch (start us, length us, event | category | flops | bytes accessed | tf_op | source)
XLA Modules:
  0.0 14.0 jit_solution(16990229615160188198)
XLA Ops:
  0.0 13.2 %shard_map.37 = f32[4,16,8,128]{3,2,1,0:T(8,128)S(1)} custom-call(f32[4,16,8,128]{3,2,1,0:T(8,128)} %fields.1, s32[8,16]{1,0:T(8,128)} %bitcast.2, f32[8,16]{1,0:T(8,128)} %bitcast.3), custom_call_target="tpu_custom_call" | custom-call | tf_op jit(solution)/shard_map/pallas_call | solution.py:310
  13.3 0.7 %copy.5 = f32[4,16,8,128]{3,2,1,0:T(8,128)} copy(f32[4,16,8,128]{3,2,1,0:T(8,128)S(1)} %shard_map.37) | data formatting | bytes 524288

commit v2 on v1

--- a/solution.py
+++ b/solution.py
@@ -12,7 +12,7 @@
 adiabatic = 1.4
 MESH = pl.DeviceIdType.MESH
 OFFSETS = (-2, -1, 0, 1)
-BOUNDS = (0, 4, 9, 13, 15, 16)
+BOUNDS = (0, 8, 14, 16)
 
 
 def remote(src, dst, send, recv, az, rad):
@@ -31,8 +31,8 @@
 
 
 def kernel(n, rn, bounds, fields, shifts_in, courant_in, out, raw, early, G, H, ZS, ZR, FX, SEG, LANE, CA, shifts, courant,
-           local_sem, small_sem, sent, edge_sent, edge_got, side_sent, side_got, fix_sent, fix_got, dens_got, dens_mate, got, mate_got):
-    _, T, R, L = fields.shape
+           local_sem, small_sem, sent, aux_sent, halo_got, fix_got, dens_got, got, mate_got):
+    F, T, R, L = fields.shape
     X = n // 2
     K = len(bounds) - 1
     fill = bounds[1]
@@ -42,6 +42,13 @@
     mate = x * 2 + (1 - c)
     before, after = lax.rem(az + n - 1, n), lax.rem(az + 1, n)
 
+    def tiles(m):
+        for a in range(1, n + 1):
+            for b in range(1, F + 1):
+                if m % (a * b) == 0 and m // (a * b) <= T:
+                    return G.at[pl.ds(0, a), pl.ds(0, b), pl.ds(0, m // (a * b))]
+        raise ValueError(m)
+
     def column(k, core=None):
         return lax.rem(x + k, X) * 2 + (c if core is None else core)
 
@@ -72,8 +79,8 @@
         pltpu.make_async_copy(courant_in, courant, small_sem.at[1]),
     )
     local = (
-        pltpu.make_async_copy(fields.at[0:3], raw, local_sem.at[0]),
-        pltpu.make_async_copy(fields.at[3], G.at[az, 3], local_sem.at[1]),
+        pltpu.make_async_copy(fields.at[0:3], raw, local_sem),
+        pltpu.make_async_copy(fields.at[3], G.at[az, 3], local_sem),
     )
     for copy in small + local:
         copy.start()
@@ -124,8 +131,7 @@
             SEG[t, o] = jnp.where(seg < 0, seg + n, seg)
             LANE[t, o] = (lane - rest) & (L - 1)
 
-    for copy in local:
-        copy.wait()
+    pltpu.make_async_copy(fields, G.at[0], local_sem).wait()
 
     for side in range(2):
         for p in range(ZS.shape[1]):
@@ -171,17 +177,14 @@
         )
         dst[2, t] = en - en * (heat_rad * (vu - vd) + heat_az * (ph - pl_) + heat_r * vr)
 
-    for t in range(fill):
-        stencil(t, early, True)
-
     neighbours = has_low.astype(jnp.int32) + has_high.astype(jnp.int32)
     pl.semaphore_wait(barrier, 2 * X - 1 + neighbours)
 
     def side_copy(side):
-        return remote(ZS.at[side], ZR.at[1 - side], side_sent, side_got, after if side else before, rad)
+        return remote(ZS.at[side], ZR.at[1 - side], aux_sent, halo_got, after if side else before, rad)
 
     def edge_copy(way):
-        return remote(raw.at[:, :, (R - 1) * (1 - way), :], H.at[way], edge_sent.at[way], edge_got.at[way], az, toward[way])
+        return remote(raw.at[:, :, (R - 1) * (1 - way), :], H.at[way], aux_sent, halo_got, az, toward[way])
 
     def block(seg, j):
         return G.at[seg, 0:3, pl.ds(bounds[j], bounds[j + 1] - bounds[j])]
@@ -194,18 +197,19 @@
             edge_copy(way).start()
     for k in range(1, X):
         remote(G.at[az, 3], G.at[az, 3], sent, dens_got.at[k - 1], column(k), rad).start()
+    for t in range(fill):
+        stencil(t, early, True)
+
     for k in range(1, X):
         inside = pl.ds(1, R - 2)
         remote(early.at[:, :, inside], G.at[az, 0:3, pl.ds(0, fill), inside], sent, got.at[0, k - 1], column(k), rad).start()
-    remote(G.at[az, 3], G.at[az, 3], sent, dens_mate, mate, rad).start()
-
-    remote(ZR, ZR, side_sent, side_got, mate, rad).wait_recv()
-    for way in range(2):
-        @pl.when(receives[way])
-        def _():
-            remote(H.at[way], H.at[way], edge_sent.at[way], edge_got.at[way], az, rad).wait_recv()
-
-    for j in [1, 0] + list(range(2, K)):
+    for count in range(3):
+        @pl.when(neighbours == count)
+        def _():
+            came = tiles(2 * ZR.shape[1] + count * 3 * T // R)
+            remote(came, came, aux_sent, halo_got, mate, rad).wait_recv()
+
+    for j in range(K):
         for t in range(bounds[j], bounds[j + 1]):
             stencil(t, G.at[az], False)
         if j == 0:
@@ -219,12 +223,14 @@
                 for r in (0, R - 1):
                     line = G.at[az, 0:3, pl.ds(0, fill), r]
                     remote(line, line, sent, got.at[0, k - 1], column(k), rad).start()
-                remote(FX.at[az], FX.at[az], fix_sent, fix_got.at[k - 1], column(k), rad).start()
+                remote(FX.at[az], FX.at[az], aux_sent, fix_got.at[k - 1], column(k), rad).start()
         else:
             for k in range(1, X):
                 remote(block(az, j), block(az, j), sent, got.at[j, k - 1], column(k), rad).start()
                 if j == K - 1:
                     remote(block(az, j), block(az, j), sent, mate_got.at[j], column(k, 1 - c), rad).start()
+    remote(G.at[az, 3], G.at[az, 3], sent, mate_got.at[0], mate, rad).start()
+    for j in range(K):
         remote(block(az, j), block(az, j), sent, mate_got.at[j], mate, rad).start()
 
     def step(t):
@@ -253,7 +259,7 @@
             copy = remote(block(seg, j), block(seg, j), sent, got.at[j, k - 1], mate, rad)
             copy.wait_recv()
             if j == 0:
-                remote(FX.at[seg], FX.at[seg], fix_sent, fix_got.at[k - 1], mate, rad).wait_recv()
+                remote(FX.at[seg], FX.at[seg], aux_sent, fix_got.at[k - 1], mate, rad).wait_recv()
                 for i in range(3 * fill):
                     f, t = i // fill, i % fill
                     p, at = 2 * i // L, 2 * i % L
@@ -263,8 +269,8 @@
                 remote(block(seg, j), block(seg, j), sent, mate_got.at[j], mate, rad).start()
 
     def finish(j):
-        every = G.at[pl.ds(0, X), 0:3, pl.ds(0, bounds[j + 1] - bounds[j])]
-        remote(every, every, sent, mate_got.at[j], mate, rad).wait_recv()
+        came = tiles(X * (3 * (bounds[j + 1] - bounds[j]) + (0 if j else T)))
+        remote(came, came, sent, mate_got.at[j], mate, rad).wait_recv()
 
         for t in range(bounds[j], bounds[j + 1]):
             step(t)
@@ -273,26 +279,24 @@
         seg = source(k, c)
         copy = remote(G.at[seg, 3], G.at[seg, 3], sent, dens_got.at[k - 1], mate, rad)
         copy.wait_recv()
-        remote(G.at[seg, 3], G.at[seg, 3], sent, dens_mate, mate, rad).start()
+        remote(G.at[seg, 3], G.at[seg, 3], sent, mate_got.at[0], mate, rad).start()
+    take(0)
     take(1)
-    take(0)
-    dens = G.at[pl.ds(0, X), 3]
-    remote(dens, dens, sent, dens_mate, mate, rad).wait_recv()
-    order = [1, 0] + list(range(2, K))
-    for i, j in enumerate(order):
-        if i > 0 and i + 1 < K:
-            take(order[i + 1])
+    for j in range(K - 2):
+        if j > 0:
+            take(j + 1)
         finish(j)
-
-    for way in range(2):
-        @pl.when(sends[way])
-        def _():
-            edge_copy(way).wait_send()
-    remote(ZS, ZS, side_sent, side_got, mate, rad).wait_send()
-    fixes = FX.at[pl.ds(0, X - 1)]
-    remote(fixes, fixes, fix_sent, side_got, mate, rad).wait_send()
+    take(K - 1)
+    finish(K - 1)
+    finish(K - 2)
+
+    for count in range(3):
+        @pl.when(neighbours == count)
+        def _():
+            gone = tiles(2 * ZR.shape[1] + (X - 1) * FX.shape[1] + count * 3 * T // R)
+            remote(gone, gone, aux_sent, halo_got, mate, rad).wait_send()
     every = G.at[pl.ds(0, 2 * X - 1)]
-    remote(every, every, sent, side_got, mate, rad).wait_send()
+    remote(every, every, sent, halo_got, mate, rad).wait_send()
 
 
 def shards(fields, shifts, courant):
@@ -325,9 +329,8 @@
             pltpu.VMEM((T, R, L), jnp.float32),
             pltpu.VMEM((R, T), jnp.int32),
             pltpu.VMEM((R, T), jnp.float32),
-            dma((2,)), dma((2,)),
-            dma(()), dma((2,)), dma((2,)), dma(()), dma(()), dma(()), dma((X - 1,)),
-            dma((X - 1,)), dma(()), dma((K, X - 1)), dma((K,)),
+            dma(()), dma((2,)), dma(()), dma(()), dma(()),
+            dma((X - 1,)), dma((X - 1,)), dma((K, X - 1)), dma((K,)),
         ],
         compiler_params=pltpu.CompilerParams(collective_id=0, has_side_effects=True, vmem_limit_bytes=grant),
     )(*(pltpu.with_memory_space_constraint(v, pltpu.HBM) for v in (fields, shifts.T, courant.T)))

time: 14.1 us -> 12.7 us (0.901)
  the two profiles are of different devices: /device:TPU:0 before, /device:TPU:1 now
where the time goes in v2:
time: 12.7 us; the launch traced here: 12.6 us
  Pallas kernels  11.9 us (94%)
  local copies, waits for them, and re-layouts  0.71 us (6%)
    pallas_call x1, Pallas kernels, shards(): pl.pallas_call(functools.partial(kernel, n, rn, bounds), out_shape=jax.Sh...  11.9 us
    unnamed x1, local copies, waits for them, and re-layouts  0.71 us

profile of v2, /device:TPU:1, one launch (start us, length us, event | category | flops | bytes accessed | tf_op | source)
XLA Modules:
  0.0 12.6 jit_solution(6758318677076849426)
XLA Ops:
  0.0 11.9 %shard_map.37 = f32[4,16,8,128]{3,2,1,0:T(8,128)S(1)} custom-call(f32[4,16,8,128]{3,2,1,0:T(8,128)} %fields.1, s32[8,16]{1,0:T(8,128)} %bitcast.2, f32[8,16]{1,0:T(8,128)} %bitcast.3), custom_call_target="tpu_custom_call" | custom-call | tf_op jit(solution)/shard_map/pallas_call | solution.py:314
  11.9 0.7 %copy.5 = f32[4,16,8,128]{3,2,1,0:T(8,128)} copy(f32[4,16,8,128]{3,2,1,0:T(8,128)S(1)} %shard_map.37) | data formatting | bytes 524288

commit v3 on v2

v3 whole, which is shorter than its diff:
```python
import functools
import math

import jax
import jax.numpy as jnp
from jax import lax
from jax.experimental import pallas as pl
from jax.experimental.pallas import tpu as pltpu
from jax.sharding import PartitionSpec as P

inner_radius = 0.4
adiabatic = 1.4
MESH = pl.DeviceIdType.MESH
OFFSETS = (-2, -1, 0, 1)
BOUNDS = (0, 8, 12, 16)


def remote(src, dst, send, recv, az, rad):
    return pltpu.make_async_remote_copy(
        src_ref=src,
        dst_ref=dst,
        send_sem=send,
        recv_sem=recv,
        device_id={"az": az, "rad": rad},
        device_id_type=MESH,
    )


def minmod(a, b):
    return jnp.maximum(jnp.minimum(a, b), 0.0) + jnp.minimum(jnp.maximum(a, b), 0.0)


def kernel(n, rn, bounds, fields, shifts_in, courant_in, out, raw, early, D, G, H, ZS, ZR, FX, SEG, LANE, CA, shifts, courant,
           local_sem, small_sem, sent, aux_sent, halo_got, got, mate_got):
    _, T, R, L = fields.shape
    X = n // 2
    K = len(bounds) - 1
    fill = bounds[1]
    az = lax.axis_index("az")
    rad = lax.axis_index("rad")
    x, c = az // 2, az % 2
    mate = x * 2 + (1 - c)
    before, after = lax.rem(az + n - 1, n), lax.rem(az + 1, n)

    def column(k, core=None):
        return lax.rem(x + k, X) * 2 + (c if core is None else core)

    def source(k, core):
        return lax.rem(x + X - k, X) * 2 + core

    def tiles(m):
        return G.at[pl.ds(0, m)]

    def dens(seg):
        return D.at[pl.ds(seg * T, T)]

    has_low, has_high = rad > 0, rad < rn - 1
    sends = (has_high, has_low)
    receives = (has_low, has_high)
    toward = (rad + 1, rad - 1)
    neighbours = has_low.astype(jnp.int32) + has_high.astype(jnp.int32)

    barrier = pltpu.get_barrier_semaphore()

    def greet(sem, a, r):
        pl.semaphore_signal(sem, inc=1, device_id={"az": a, "rad": r}, device_id_type=MESH)

    greet(barrier, mate, rad)
    for k in range(1, X):
        greet(barrier, column(k), rad)
        greet(barrier, column(k, 1 - c), rad)
    for way in range(2):
        @pl.when(sends[way])
        def _():
            greet(barrier, az, toward[way])

    small = (
        pltpu.make_async_copy(shifts_in, shifts, small_sem),
        pltpu.make_async_copy(courant_in, courant.at[0], small_sem),
    )
    local = (
        pltpu.make_async_copy(fields.at[0:3], raw, local_sem),
        pltpu.make_async_copy(fields.at[3], dens(az), local_sem),
    )
    for copy in small + local:
        copy.start()

    def density_out(from_ref):
        for k in range(1, X):
            remote(from_ref, dens(az), aux_sent, got.at[0, k - 1], column(k), rad).start()

    def edge_copy(way, from_ref):
        return remote(from_ref.at[:, :, (R - 1) * (1 - way), :], H.at[way], aux_sent, halo_got, az, toward[way])

    def edges_out(rows):
        for way in range(2):
            pl.when(sends[way])(edge_copy(way, rows).start)

    phi_count, rad_count = n * L, rn * R
    phi_step = 2.0 * math.pi / phi_count
    rad_step = 1.0 / rad_count
    spacing = min(rad_step, inner_radius * phi_step)
    dt = 0.2 * spacing
    viscosity = 0.05 * spacing * spacing / dt
    row = lax.broadcasted_iota(jnp.int32, (R, L), 0)
    lane = lax.broadcasted_iota(jnp.int32, (R, L), 1)
    radius = inner_radius + ((rad * R + row).astype(jnp.float32) + 0.5) * (1.0 / rad_count)
    width = radius * phi_step
    inv_r = 1.0 / radius
    inv_w = 1.0 / width
    spread_az = (dt * viscosity) * inv_w * inv_w
    spread_rad = dt * viscosity / (rad_step * rad_step)
    press_rad = dt * (adiabatic - 1.0) * 0.5 / rad_step
    press_az = (dt * (adiabatic - 1.0) * 0.5) * inv_w
    turn = dt * inv_r
    pull = dt * inv_r * inv_r
    heat = dt * (adiabatic - 1.0)
    heat_rad = heat * 0.5 / rad_step
    heat_az = (heat * 0.5) * inv_w
    heat_r = heat * inv_r
    bits = L.bit_length() - 1
    first_lane, last_lane = lane == 0, lane == L - 1
    first_row, last_row = row == 0, row == R - 1

    def turned(value, amount):
        return pltpu.roll(value, amount % L, 1) if amount % L else value

    pltpu.make_async_copy(tiles(4 * T), tiles(4 * T), local_sem).wait()

    for side in range(2):
        for p in range(ZS.shape[1]):
            packed = jnp.zeros((R, L), jnp.float32)
            for i in range(p * L, min(3 * T, (p + 1) * L)):
                packed = jnp.where(lane == i - p * L, turned(raw[i // T, i % T], i - p * L + side), packed)
            ZS[side, p] = packed

    for way in range(2):
        @pl.when(jnp.logical_not(receives[way]))
        def _():
            H[way] = raw[:, :, (R - 1) * way, :]

    def stencil(t, inner):
        vr, vp, en, den = raw[0, t], raw[1, t], raw[2, t], D[az * T + t]

        def around(f, q):
            i = f * T + t
            left, right = turned(q, 1), turned(q, L - 1)
            low, high = pltpu.roll(q, 1, 0), pltpu.roll(q, R - 1, 0)
            if not inner:
                left = jnp.where(first_lane, turned(ZR[0, i // L], -i), left)
                right = jnp.where(last_lane, turned(ZR[1, i // L], L - 1 - i), right)
                low = jnp.where(first_row, H[0, f, pl.ds(t, 1), :], low)
                high = jnp.where(last_row, H[1, f, pl.ds(t, 1), :], high)
            return left, right, low, high

        vl, vh, vd, vu = around(0, vr)
        pl_, ph, pd, pu = around(1, vp)
        el, eh, ed, eu = around(2, en)
        inv_den = 1.0 / den
        new_r = vr + (
            spread_az * (vh + vl - 2.0 * vr)
            + spread_rad * (vu + vd - 2.0 * vr)
            + (vp * vp * turn - pull)
            - press_rad * (eu - ed) * inv_den
        )
        new_p = vp + (
            spread_az * (ph + pl_ - 2.0 * vp)
            + spread_rad * (pu + pd - 2.0 * vp)
            - vr * vp * turn
            - press_az * (eh - el) * inv_den
        )
        new_e = en - en * (heat_rad * (vu - vd) + heat_az * (ph - pl_) + heat_r * vr)
        return new_r, new_p, new_e

    def place(seg, t):
        return (seg * T + t) * 3

    def block(seg, j):
        return G.at[pl.ds(place(seg, bounds[j]), 3 * (bounds[j + 1] - bounds[j]))]

    def side_copy(side):
        return remote(ZS.at[side], ZR.at[1 - side], aux_sent, halo_got, after if side else before, rad)

    pl.semaphore_wait(barrier, 2 * X - 1 + neighbours)

    for side in range(2):
        side_copy(side).start()

    edges_out(raw)

    density_out(dens(az))

    for t in range(fill):
        for f, value in enumerate(stencil(t, True)):
            early[3 * t + f] = value
    for k in range(1, X):
        inside = pl.ds(1, R - 2)
        remote(early.at[:, inside], G.at[pl.ds(place(az, 0), 3 * fill), inside], sent, got.at[0, k - 1], column(k), rad).start()

    pltpu.make_async_copy(courant, courant, small_sem).wait()
    for t in range(T):
        moves = jnp.broadcast_to(shifts[:, t : t + 1], (R, L))
        cour = jnp.broadcast_to(courant[0, :, t : t + 1], (R, L))
        CA[t] = jnp.abs(cour)
        sign = jnp.where(cour >= 0.0, 1, -1)
        for o, offset in enumerate(OFFSETS):
            s = moves - sign * offset
            s = jnp.where(s < 0, s + phi_count, s)
            s = jnp.where(s >= phi_count, s - phi_count, s)
            q = s >> bits
            rest = s & (L - 1)
            seg = az - q - jnp.where(lane + rest >= L, 1, 0)
            SEG[t, o] = jnp.where(seg < 0, seg + n, seg)
            LANE[t, o] = (lane - rest) & (L - 1)

    for count in range(3):
        @pl.when(neighbours == count)
        def _():
            came = tiles(2 * ZR.shape[1] + count * 3 * T // R)
            remote(came, came, aux_sent, halo_got, mate, rad).wait_recv()

    for j in range(K):
        for t in range(bounds[j], bounds[j + 1]):
            for f, value in enumerate(stencil(t, False)):
                G[place(az, t) + f] = value
        if j == 0:
            for p in range(FX.shape[1]):
                packed = jnp.zeros((R, L), jnp.float32)
                for i in range(p * L, min(6 * fill, (p + 1) * L)):
                    packed = jnp.where(lane == i - p * L, turned(G[place(az, 0) + i // 2], i - p * L + i % 2), packed)
                FX[az, p] = packed
            for k in range(1, X):
                for r in (0, R - 1):
                    line = G.at[pl.ds(place(az, 0), 3 * fill), r]
                    remote(line, line, sent, got.at[0, k - 1], column(k), rad).start()
                remote(FX.at[az], FX.at[az], aux_sent, got.at[0, k - 1], column(k), rad).start()
        else:
            for k in range(1, X):
                remote(block(az, j), block(az, j), sent, got.at[j, k - 1], column(k), rad).start()
                if j == K - 1:
                    direct = remote(block(az, j), block(az, j), sent, mate_got.at[j], column(k, 1), rad)
                    pl.when(c == 0)(direct.start)
    remote(dens(az), dens(az), aux_sent, mate_got.at[0], mate, rad).start()
    for j in range(K):
        remote(block(az, j), block(az, j), sent, mate_got.at[j], mate, rad).start()

    def step(t):
        amount = CA[t]
        half = 0.5 * (1.0 - amount)
        taken = [[] for _ in range(4)]
        moved = [[G[place(s, t) + f] for f in range(3)] + [D[s * T + t]] for s in range(n)]
        for o in range(len(OFFSETS)):
            seg, at = SEG[t, o], LANE[t, o]
            chosen = [seg == s for s in range(n - 1)]
            for f in range(4):
                value = moved[n - 1][f]
                for s in range(n - 1):
                    value = jnp.where(chosen[s], moved[s][f], value)
                taken[f].append(jnp.take_along_axis(value, at, axis=1, mode="promise_in_bounds"))
        for f in range(4):
            q0, q1, q2, q3 = taken[f]
            d0, d1, d2 = q1 - q0, q2 - q1, q3 - q2
            enters = q1 + half * minmod(d0, d1)
            leaves = q2 + half * minmod(d1, d2)
            out[f, t] = q2 - amount * (leaves - enters)

    def take(j, forward=True):
        for k in range(1, X):
            seg = source(k, c)
            came = tiles(3 * (bounds[j + 1] - bounds[j]) + (0 if j else T + FX.shape[1]))
            remote(came, came, sent, got.at[j, k - 1], mate, rad).wait_recv()
            if j == 0:
                for i in range(3 * fill):
                    p, at = 2 * i // L, 2 * i % L
                    value = jnp.where(first_lane, turned(FX[seg, p], -at), G[place(seg, 0) + i])
                    G[place(seg, 0) + i] = jnp.where(last_lane, turned(FX[seg, p], L - 2 - at), value)
                remote(dens(seg), dens(seg), aux_sent, mate_got.at[0], mate, rad).start()
            if forward:
                remote(block(seg, j), block(seg, j), sent, mate_got.at[j], mate, rad).start()

    def finish(j):
        came = tiles(X * (3 * (bounds[j + 1] - bounds[j]) + (0 if j else T)))
        remote(came, came, sent, mate_got.at[j], mate, rad).wait_recv()
        for t in range(bounds[j], bounds[j + 1]):
            step(t)

    @pl.when(c == 1)
    def _():
        for j in range(K):
            take(j)

    for j in range(K):
        @pl.when(c == 0)
        def _():
            take(j, j < K - 1)

        finish(j)

    for count in range(3):
        @pl.when(neighbours == count)
        def _():
            gone = tiles(2 * ZR.shape[1] + (2 * X - 1) * T + (X - 1) * FX.shape[1] + count * 3 * T // R)
            remote(gone, gone, aux_sent, halo_got, mate, rad).wait_send()
    gone = tiles((2 * X - 1) * 3 * T)
    remote(gone, gone, sent, halo_got, mate, rad).wait_send()


def shards(fields, shifts, courant):
    n, rn = lax.axis_size("az"), lax.axis_size("rad")
    F, T, R, L = fields.shape
    X = n // 2
    bounds = sorted({T * b // BOUNDS[-1] for b in BOUNDS})
    K, fill = len(bounds) - 1, bounds[1]
    packs, fixes = -(-3 * T // L), -(-6 * fill // L)
    tile = R * L
    held = (n + 2) * F * T * tile + 3 * fill * tile + 2 * 3 * T * L + (4 * packs + n * fixes) * tile + 9 * T * tile
    grant = 4 * held + (2 << 20)
    dma = pltpu.SemaphoreType.DMA
    vmem = pl.BlockSpec(memory_space=pltpu.VMEM)
    return pl.pallas_call(
        functools.partial(kernel, n, rn, bounds),
        out_shape=jax.ShapeDtypeStruct(fields.shape, jnp.float32),
        in_specs=[pl.BlockSpec(memory_space=pltpu.HBM)] * 3,
        out_specs=vmem,
        scratch_shapes=[
            pltpu.VMEM((3, T, R, L), jnp.float32),
            pltpu.VMEM((3 * fill, R, L), jnp.float32),
            pltpu.VMEM((n * T, R, L), jnp.float32),
            pltpu.VMEM((n * T * 3, R, L), jnp.float32),
            pltpu.VMEM((2, 3, T, L), jnp.float32),
            pltpu.VMEM((2, packs, R, L), jnp.float32),
            pltpu.VMEM((2, packs, R, L), jnp.float32),
            pltpu.VMEM((n, fixes, R, L), jnp.float32),
            pltpu.VMEM((T, 4, R, L), jnp.int32),
            pltpu.VMEM((T, 4, R, L), jnp.int32),
            pltpu.VMEM((T, R, L), jnp.float32),
            pltpu.VMEM((R, T), jnp.int32),
            pltpu.VMEM((2, R, T), jnp.float32),
            dma(()), dma(()), dma(()), dma(()), dma(()),
            dma((K, X - 1)), dma((K,)),
        ],
        compiler_params=pltpu.CompilerParams(collective_id=0, has_side_effects=True, vmem_limit_bytes=grant),
    )(*(pltpu.with_memory_space_constraint(v, pltpu.HBM) for v in (fields, shifts.T, courant.T)))


def solution(mesh):
    return jax.shard_map(
        shards,
        mesh=mesh,
        in_specs=(P(None, None, "rad", "az"), P(None, "rad"), P(None, "rad")),
        out_specs=P(None, None, "rad", "az"),
        check_vma=False,
    )
```

time: 12.7 us -> 12.6 us (level)
  Pallas kernels: 11.9 us -> 11.7 us
    pallas_call x1, Pallas kernels: 11.9 us -> 11.7 us  [shards(): pl.pallas_call(functools.partial(kernel, n, rn, bounds), out_shape=jax.Sh...]
where the time goes in v3:
time: 12.6 us; the launch traced here: 12.4 us
  Pallas kernels  11.7 us (93%)
  local copies, waits for them, and re-layouts  0.71 us (6%)
    pallas_call x1, Pallas kernels, shards(): pl.pallas_call(functools.partial(kernel, n, rn, bounds), out_shape=jax.Sh...  11.7 us
    unnamed x1, local copies, waits for them, and re-layouts  0.71 us

profile of v3, /device:TPU:1, one launch (start us, length us, event | category | flops | bytes accessed | tf_op | source)
XLA Modules:
  0.0 12.4 jit_solution(16684737382488141916)
XLA Ops:
  0.0 11.7 %shard_map.37 = f32[4,16,8,128]{3,2,1,0:T(8,128)S(1)} custom-call(f32[4,16,8,128]{3,2,1,0:T(8,128)} %fields.1, s32[8,16]{1,0:T(8,128)} %bitcast.2, f32[8,16]{1,0:T(8,128)} %bitcast.3), custom_call_target="tpu_custom_call" | custom-call | tf_op jit(solution)/shard_map/pallas_call | solution.py:320
  11.7 0.7 %copy.5 = f32[4,16,8,128]{3,2,1,0:T(8,128)} copy(f32[4,16,8,128]{3,2,1,0:T(8,128)S(1)} %shard_map.37) | data formatting | bytes 524288

commit v4 on v3

--- a/solution.py
+++ b/solution.py
@@ -12,7 +12,7 @@
 adiabatic = 1.4
 MESH = pl.DeviceIdType.MESH
 OFFSETS = (-2, -1, 0, 1)
-BOUNDS = (0, 8, 12, 16)
+BOUNDS = (0, 8, 11, 16)
 
 
 def remote(src, dst, send, recv, az, rad):
@@ -27,11 +27,11 @@
 
 
 def minmod(a, b):
-    return jnp.maximum(jnp.minimum(a, b), 0.0) + jnp.minimum(jnp.maximum(a, b), 0.0)
+    return jnp.maximum(jnp.minimum(a, b), jnp.minimum(jnp.maximum(a, b), 0.0))
 
 
 def kernel(n, rn, bounds, fields, shifts_in, courant_in, out, raw, early, D, G, H, ZS, ZR, FX, SEG, LANE, CA, shifts, courant,
-           local_sem, small_sem, sent, aux_sent, halo_got, got, mate_got):
+           local_sem, small_sem, sent, aux_sent, halo_got, late_got, dens_got, got, mate_got):
     _, T, R, L = fields.shape
     X = n // 2
     K = len(bounds) - 1
@@ -87,14 +87,18 @@
 
     def density_out(from_ref):
         for k in range(1, X):
-            remote(from_ref, dens(az), aux_sent, got.at[0, k - 1], column(k), rad).start()
-
-    def edge_copy(way, from_ref):
-        return remote(from_ref.at[:, :, (R - 1) * (1 - way), :], H.at[way], aux_sent, halo_got, az, toward[way])
-
-    def edges_out(rows):
-        for way in range(2):
-            pl.when(sends[way])(edge_copy(way, rows).start)
+            remote(from_ref, dens(az), aux_sent, dens_got.at[k - 1], column(k), rad).start()
+
+    parts = ((0, fill, halo_got), (fill, T - fill, late_got))
+
+    def edge_copy(way, first, count, got_sem):
+        some = pl.ds(first, count)
+        return remote(raw.at[:, some, (R - 1) * (1 - way), :], H.at[way, :, some], aux_sent, got_sem, az, toward[way])
+
+    def edges_out():
+        for part in parts:
+            for way in range(2):
+                pl.when(sends[way])(edge_copy(way, *part).start)
 
     phi_count, rad_count = n * L, rn * R
     phi_step = 2.0 * math.pi / phi_count
@@ -186,7 +190,7 @@
     for side in range(2):
         side_copy(side).start()
 
-    edges_out(raw)
+    edges_out()
 
     density_out(dens(az))
 
@@ -216,10 +220,17 @@
     for count in range(3):
         @pl.when(neighbours == count)
         def _():
-            came = tiles(2 * ZR.shape[1] + count * 3 * T // R)
+            came = tiles(2 * ZR.shape[1] + count * 3 * fill // R)
             remote(came, came, aux_sent, halo_got, mate, rad).wait_recv()
 
     for j in range(K):
+        if j == 1:
+            for count in range(1, 3):
+                @pl.when(neighbours == count)
+                def _():
+                    came = tiles(count * 3 * (T - fill) // R)
+                    remote(came, came, aux_sent, late_got, mate, rad).wait_recv()
+
         for t in range(bounds[j], bounds[j + 1]):
             for f, value in enumerate(stencil(t, False)):
                 G[place(az, t) + f] = value
@@ -267,14 +278,13 @@
     def take(j, forward=True):
         for k in range(1, X):
             seg = source(k, c)
-            came = tiles(3 * (bounds[j + 1] - bounds[j]) + (0 if j else T + FX.shape[1]))
+            came = tiles(3 * (bounds[j + 1] - bounds[j]) + (0 if j else FX.shape[1]))
             remote(came, came, sent, got.at[j, k - 1], mate, rad).wait_recv()
             if j == 0:
                 for i in range(3 * fill):
                     p, at = 2 * i // L, 2 * i % L
                     value = jnp.where(first_lane, turned(FX[seg, p], -at), G[place(seg, 0) + i])
                     G[place(seg, 0) + i] = jnp.where(last_lane, turned(FX[seg, p], L - 2 - at), value)
-                remote(dens(seg), dens(seg), aux_sent, mate_got.at[0], mate, rad).start()
             if forward:
                 remote(block(seg, j), block(seg, j), sent, mate_got.at[j], mate, rad).start()
 
@@ -283,6 +293,11 @@
         remote(came, came, sent, mate_got.at[j], mate, rad).wait_recv()
         for t in range(bounds[j], bounds[j + 1]):
             step(t)
+
+    for k in range(1, X):
+        seg = source(k, c)
+        remote(dens(seg), dens(seg), aux_sent, dens_got.at[k - 1], mate, rad).wait_recv()
+        remote(dens(seg), dens(seg), aux_sent, mate_got.at[0], mate, rad).start()
 
     @pl.when(c == 1)
     def _():
@@ -336,8 +351,8 @@
             pltpu.VMEM((T, R, L), jnp.float32),
             pltpu.VMEM((R, T), jnp.int32),
             pltpu.VMEM((2, R, T), jnp.float32),
-            dma(()), dma(()), dma(()), dma(()), dma(()),
-            dma((K, X - 1)), dma((K,)),
+            dma(()), dma(()), dma(()), dma(()), dma(()), dma(()),
+            dma((X - 1,)), dma((K, X - 1)), dma((K,)),
         ],
         compiler_params=pltpu.CompilerParams(collective_id=0, has_side_effects=True, vmem_limit_bytes=grant),
     )(*(pltpu.with_memory_space_constraint(v, pltpu.HBM) for v in (fields, shifts.T, courant.T)))

time: 12.6 us -> 12.4 us (0.984)
  Pallas kernels: 11.7 us -> 11.5 us
    pallas_call x1, Pallas kernels: 11.7 us -> 11.5 us  [shards(): pl.pallas_call(functools.partial(kernel, n, rn, bounds), out_shape=jax.Sh...]
where the time goes in v4:
time: 12.4 us; the launch traced here: 12.2 us
  Pallas kernels  11.5 us (93%)
  local copies, waits for them, and re-layouts  0.71 us (6%)
    pallas_call x1, Pallas kernels, shards(): pl.pallas_call(functools.partial(kernel, n, rn, bounds), out_shape=jax.Sh...  11.5 us
    unnamed x1, local copies, waits for them, and re-layouts  0.71 us

profile of v4, /device:TPU:1, one launch (start us, length us, event | category | flops | bytes accessed | tf_op | source)
XLA Modules:
  0.0 12.2 jit_solution(14319806210037572622)
XLA Ops:
  0.0 11.5 %shard_map.37 = f32[4,16,8,128]{3,2,1,0:T(8,128)S(1)} custom-call(f32[4,16,8,128]{3,2,1,0:T(8,128)} %fields.1, s32[8,16]{1,0:T(8,128)} %bitcast.2, f32[8,16]{1,0:T(8,128)} %bitcast.3), custom_call_target="tpu_custom_call" | custom-call | tf_op jit(solution)/shard_map/pallas_call | solution.py:335
  11.5 0.7 %copy.5 = f32[4,16,8,128]{3,2,1,0:T(8,128)} copy(f32[4,16,8,128]{3,2,1,0:T(8,128)S(1)} %shard_map.37) | data formatting | bytes 524288

commit v5 on v4

--- a/solution.py
+++ b/solution.py
@@ -97,7 +97,7 @@
 
     def edges_out():
         for part in parts:
-            for way in range(2):
+            for way in (1, 0):
                 pl.when(sends[way])(edge_copy(way, *part).start)
 
     phi_count, rad_count = n * L, rn * R
@@ -187,10 +187,10 @@
 
     pl.semaphore_wait(barrier, 2 * X - 1 + neighbours)
 
+    edges_out()
+
     for side in range(2):
         side_copy(side).start()
-
-    edges_out()
 
     density_out(dens(az))
 
@@ -235,15 +235,16 @@
             for f, value in enumerate(stencil(t, False)):
                 G[place(az, t) + f] = value
         if j == 0:
+            for k in range(1, X):
+                for r in (0, R - 1):
+                    line = G.at[pl.ds(place(az, 0), 3 * fill), r]
+                    remote(line, line, sent, got.at[0, k - 1], column(k), rad).start()
             for p in range(FX.shape[1]):
                 packed = jnp.zeros((R, L), jnp.float32)
                 for i in range(p * L, min(6 * fill, (p + 1) * L)):
                     packed = jnp.where(lane == i - p * L, turned(G[place(az, 0) + i // 2], i - p * L + i % 2), packed)
                 FX[az, p] = packed
             for k in range(1, X):
-                for r in (0, R - 1):
-                    line = G.at[pl.ds(place(az, 0), 3 * fill), r]
-                    remote(line, line, sent, got.at[0, k - 1], column(k), rad).start()
                 remote(FX.at[az], FX.at[az], aux_sent, got.at[0, k - 1], column(k), rad).start()
         else:
             for k in range(1, X):
@@ -288,11 +289,9 @@
             if forward:
                 remote(block(seg, j), block(seg, j), sent, mate_got.at[j], mate, rad).start()
 
-    def finish(j):
+    def arrive(j):
         came = tiles(X * (3 * (bounds[j + 1] - bounds[j]) + (0 if j else T)))
         remote(came, came, sent, mate_got.at[j], mate, rad).wait_recv()
-        for t in range(bounds[j], bounds[j + 1]):
-            step(t)
 
     for k in range(1, X):
         seg = source(k, c)
@@ -304,12 +303,16 @@
         for j in range(K):
             take(j)
 
-    for j in range(K):
+    for group in [(j,) for j in range(K - 2)] + [(K - 2, K - 1)]:
         @pl.when(c == 0)
         def _():
-            take(j, j < K - 1)
-
-        finish(j)
+            for j in group:
+                take(j, j < K - 1)
+
+        for j in group:
+            arrive(j)
+        for t in range(bounds[group[0]], bounds[group[-1] + 1]):
+            step(t)
 
     for count in range(3):
         @pl.when(neighbours == count)

time: 12.4 us -> 12.2 us (0.984)
    pallas_call x1, Pallas kernels: 11.5 us -> 11.4 us  [shards(): pl.pallas_call(functools.partial(kernel, n, rn, bounds), out_shape=jax.Sh...]
where the time goes in v5:
time: 12.2 us; the launch traced here: 12.1 us
  Pallas kernels  11.4 us (93%)
  local copies, waits for them, and re-layouts  0.71 us (6%)
    pallas_call x1, Pallas kernels, shards(): pl.pallas_call(functools.partial(kernel, n, rn, bounds), out_shape=jax.Sh...  11.4 us
    unnamed x1, local copies, waits for them, and re-layouts  0.71 us

profile of v5, /device:TPU:1, one launch (start us, length us, event | category | flops | bytes accessed | tf_op | source)
XLA Modules:
  0.0 12.1 jit_solution(17553557321193259195)
XLA Ops:
  0.0 11.4 %shard_map.37 = f32[4,16,8,128]{3,2,1,0:T(8,128)S(1)} custom-call(f32[4,16,8,128]{3,2,1,0:T(8,128)} %fields.1, s32[8,16]{1,0:T(8,128)} %bitcast.2, f32[8,16]{1,0:T(8,128)} %bitcast.3), custom_call_target="tpu_custom_call" | custom-call | tf_op jit(solution)/shard_map/pallas_call | solution.py:338
  11.4 0.7 %copy.5 = f32[4,16,8,128]{3,2,1,0:T(8,128)} copy(f32[4,16,8,128]{3,2,1,0:T(8,128)S(1)} %shard_map.37) | data formatting | bytes 524288

commit v6 on v5

--- a/solution.py
+++ b/solution.py
@@ -241,8 +241,9 @@
                     remote(line, line, sent, got.at[0, k - 1], column(k), rad).start()
             for p in range(FX.shape[1]):
                 packed = jnp.zeros((R, L), jnp.float32)
-                for i in range(p * L, min(6 * fill, (p + 1) * L)):
-                    packed = jnp.where(lane == i - p * L, turned(G[place(az, 0) + i // 2], i - p * L + i % 2), packed)
+                for i in range(p * L // 2, min(3 * fill, (p + 1) * L // 2)):
+                    at = 2 * i - p * L
+                    packed = jnp.where(lane >> 1 == at // 2, turned(G[place(az, 0) + i], at + 1), packed)
                 FX[az, p] = packed
             for k in range(1, X):
                 remote(FX.at[az], FX.at[az], aux_sent, got.at[0, k - 1], column(k), rad).start()
@@ -284,8 +285,7 @@
             if j == 0:
                 for i in range(3 * fill):
                     p, at = 2 * i // L, 2 * i % L
-                    value = jnp.where(first_lane, turned(FX[seg, p], -at), G[place(seg, 0) + i])
-                    G[place(seg, 0) + i] = jnp.where(last_lane, turned(FX[seg, p], L - 2 - at), value)
+                    G[place(seg, 0) + i] = jnp.where(first_lane | last_lane, turned(FX[seg, p], -at - 1), G[place(seg, 0) + i])
             if forward:
                 remote(block(seg, j), block(seg, j), sent, mate_got.at[j], mate, rad).start()
 

time: 12.2 us -> 12.2 us (level)
  no operation moved by 1% of the time
where the time goes in v6:
time: 12.2 us; the launch traced here: 12.1 us
  Pallas kernels  11.4 us (93%)
  local copies, waits for them, and re-layouts  0.71 us (6%)
    pallas_call x1, Pallas kernels, shards(): pl.pallas_call(functools.partial(kernel, n, rn, bounds), out_shape=jax.Sh...  11.4 us
    unnamed x1, local copies, waits for them, and re-layouts  0.71 us

profile of v6, /device:TPU:1, one launch (start us, length us, event | category | flops | bytes accessed | tf_op | source)
XLA Modules:
  0.0 12.1 jit_solution(16181617936449898281)
XLA Ops:
  0.0 11.4 %shard_map.37 = f32[4,16,8,128]{3,2,1,0:T(8,128)S(1)} custom-call(f32[4,16,8,128]{3,2,1,0:T(8,128)} %fields.1, s32[8,16]{1,0:T(8,128)} %bitcast.2, f32[8,16]{1,0:T(8,128)} %bitcast.3), custom_call_target="tpu_custom_call" | custom-call | tf_op jit(solution)/shard_map/pallas_call | solution.py:338
  11.4 0.7 %copy.5 = f32[4,16,8,128]{3,2,1,0:T(8,128)} copy(f32[4,16,8,128]{3,2,1,0:T(8,128)S(1)} %shard_map.37) | data formatting | bytes 524288

commit v7 on v6

--- a/solution.py
+++ b/solution.py
@@ -12,7 +12,7 @@
 adiabatic = 1.4
 MESH = pl.DeviceIdType.MESH
 OFFSETS = (-2, -1, 0, 1)
-BOUNDS = (0, 8, 11, 16)
+BOUNDS = (0, 8, 10, 16)
 
 
 def remote(src, dst, send, recv, az, rad):

time: 12.2 us -> 12.2 us (level)
  no operation moved by 1% of the time
where the time goes in v7:
time: 12.2 us; the launch traced here: 12.1 us
  Pallas kernels  11.4 us (93%)
  local copies, waits for them, and re-layouts  0.71 us (6%)
    pallas_call x1, Pallas kernels, shards(): pl.pallas_call(functools.partial(kernel, n, rn, bounds), out_shape=jax.Sh...  11.4 us
    unnamed x1, local copies, waits for them, and re-layouts  0.71 us

profile of v7, /device:TPU:1, one launch (start us, length us, event | category | flops | bytes accessed | tf_op | source)
XLA Modules:
  0.0 12.1 jit_solution(7050975133702263866)
XLA Ops:
  0.0 11.4 %shard_map.37 = f32[4,16,8,128]{3,2,1,0:T(8,128)S(1)} custom-call(f32[4,16,8,128]{3,2,1,0:T(8,128)} %fields.1, s32[8,16]{1,0:T(8,128)} %bitcast.2, f32[8,16]{1,0:T(8,128)} %bitcast.3), custom_call_target="tpu_custom_call" | custom-call | tf_op jit(solution)/shard_map/pallas_call | solution.py:338
  11.4 0.7 %copy.5 = f32[4,16,8,128]{3,2,1,0:T(8,128)} copy(f32[4,16,8,128]{3,2,1,0:T(8,128)S(1)} %shard_map.37) | data formatting | bytes 524288
